TPU v7x, 128 devices: a whole 4x4x4 slice. The times are simulated.
128 devices in a mesh: dp: 32 (over x, y, core), tensor: 4 (over z).
Axes of the slice: x: 4, y: 4, z: 4, core: 2. Of those that a mesh axis runs over, the one named last changes fastest.
Arguments:
- activations: bfloat16 [65536, 8192], P('dp', 'tensor'), may hold values from -16 to 16
- whitening: bfloat16 [8192, 1024], P('tensor'), may hold values from -8 to 8
- factor: bfloat16 [1024, 1024], P(('dp', 'tensor')), may hold values from -2 to 2
Outputs:
- new_factor: float32 [1024, 1024], P(('dp', 'tensor'))
All inputs are finite; a program needn't handle non-finite values.
Results may differ from a plain program's by a relative error of at most 0.029.
Values may be sent and summed in bfloat16 or wider, within the bound.
A program may use at most 192 MiB of HBM per device.

v0:
```python
import jax
import jax.numpy as jnp
from jax import lax
from jax.sharding import PartitionSpec as P

ridge_shift = 0.1
epsilon = 1e-06


def solve_rows(moment_rows, hadamard):
    lower = jnp.linalg.cholesky(hadamard)
    first = jax.scipy.linalg.solve_triangular(lower, moment_rows.T, lower=True)
    second = jax.scipy.linalg.solve_triangular(lower, first, lower=True, trans=1)
    return second.T


def shards(activations, whitening, factor):
    summed = lax.psum_scatter(
        jnp.dot(activations, whitening, preferred_element_type=jnp.float32).astype(jnp.bfloat16),
        "tensor",
        scatter_dimension=0,
        tiled=True,
    )
    whole_factor = lax.all_gather(factor, ("dp", "tensor"), axis=0, tiled=True)
    projected = jnp.dot(summed, whole_factor, preferred_element_type=jnp.float32)
    squared = (projected * projected).astype(jnp.bfloat16)
    moment_rows = lax.psum_scatter(
        lax.dot_general(
            summed, squared, (((0,), (0,)), ((), ())), preferred_element_type=jnp.float32
        ),
        ("dp", "tensor"),
        scatter_dimension=0,
        tiled=True,
    )
    gram = jnp.dot(whole_factor.T, whole_factor, preferred_element_type=jnp.float32)
    hadamard = gram * gram + ridge_shift * jnp.eye(gram.shape[0], dtype=jnp.float32)
    updated = solve_rows(moment_rows, hadamard)
    column_total = lax.psum(jnp.sum(updated * updated, axis=0), ("dp", "tensor"))
    scale = jnp.sqrt(column_total / whole_factor.shape[0] + epsilon)
    return updated / scale[None, :]


def solution(mesh):
    placed = (P("dp", "tensor"), P("tensor", None), P(("dp", "tensor"), None))
    return jax.shard_map(
        shards, mesh=mesh, in_specs=placed, out_specs=P(("dp", "tensor"), None), check_vma=False
    )
```

profile of v0, /device:TPU:1, one launch (start us, length us, event | category | flops | bytes accessed | tf_op | source)
XLA Modules:
  0.0 901.7 jit_solution(2923321162316526728)
XLA Ops:
  8.1 13.8 %convolution_convert_fusion = bf16[2048,1024]{1,0:T(8,128)(2,1)} fusion(bf16[2048,2048]{1,0:T(8,128)(2,1)} %param.3, bf16[2048,1024]{1,0:T(8,128)(2,1)} %param.4), kind=kOutput, calls=%fused_computation.8 | convolution fusion | flops 8592031744 | bytes 16777216 | tf_op jit(solution)/shard_map/dot_general | solution.py:19
  22.0 77.6 %all-gather.2.cloned.1.call-done = bf16[1024,1024]{1,0:T(8,128)(2,1)} async-done(((bf16[8,1024]{1,0:T(8,128)(2,1)}), bf16[1024,1024]{1,0:T(8,128)(2,1)}) %all-gather.2.cloned.1.call-update) | async-done | bytes 2097168 | tf_op jit(solution)/shard_map/all_gather | solution.py:24
  99.6 4.6 fusion.95
  104.3 2.0 copy-done
  106.2 2.4 multiply_bitcast_fusion
  108.6 5.8 copy.4
  114.4 4.5 add_multiply_fusion
  118.9 2.0 copy-done.1
  120.9 11.7 %cholesky.222 = f32[128,128]{1,0:T(8,128)S(1)} custom-call(f32[128,128]{1,0:T(8,128)S(1)} %cholesky.577), custom_call_target="Cholesky" | custom-call | tf_op jit(solution)/shard_map/jit(cholesky)/cholesky | solution.py:11
  132.6 2.5 cholesky.254
  135.1 9.8 %custom-call.66 = f32[1,128,128]{1,2,0:T(8,128)S(1)} custom-call(f32[1,128,128]{2,1,0:T(8,128)S(1)} %get-tuple-element.44), custom_call_target="InvertDiagBlocksLowerTriangular" | custom-call | tf_op jit(solution)/shard_map/jit(cholesky)/cholesky | solution.py:11
  144.9 2.3 constant_dynamic-update-slice_fusion.50
  147.3 1.5 convolution_subtract_fusion
  148.8 11.8 %cholesky.243 = f32[128,128]{1,0:T(8,128)S(1)} custom-call(f32[128,128]{1,0:T(8,128)S(1)} %cholesky.581), custom_call_target="Cholesky" | custom-call | tf_op jit(solution)/shard_map/jit(cholesky)/cholesky | solution.py:11
  160.7 5.9 fusion.1
  167.3 9.8 %custom-call.67 = f32[1,128,128]{1,2,0:T(8,128)S(1)} custom-call(f32[1,128,128]{2,1,0:T(8,128)S(1)} %get-tuple-element.41), custom_call_target="InvertDiagBlocksLowerTriangular" | custom-call | tf_op jit(solution)/shard_map/jit(cholesky)/cholesky | solution.py:11
  178.3 2.1 convolution_subtract_fusion.1
  180.4 11.7 %cholesky.466 = f32[128,128]{1,0:T(8,128)S(1)} custom-call(f32[128,128]{1,0:T(8,128)S(1)} %cholesky.586), custom_call_target="Cholesky" | custom-call | tf_op jit(solution)/shard_map/jit(cholesky)/cholesky | solution.py:11
  192.8 9.8 %custom-call.68 = f32[1,128,128]{1,2,0:T(8,128)S(1)} custom-call(f32[1,128,128]{2,1,0:T(8,128)S(1)} %get-tuple-element.38), custom_call_target="InvertDiagBlocksLowerTriangular" | custom-call | tf_op jit(solution)/shard_map/jit(cholesky)/cholesky | solution.py:11
  203.8 2.5 convolution_subtract_fusion.2
  206.3 11.7 %cholesky.485 = f32[128,128]{1,0:T(8,128)S(1)} custom-call(f32[128,128]{1,0:T(8,128)S(1)} %cholesky.591), custom_call_target="Cholesky" | custom-call | tf_op jit(solution)/shard_map/jit(cholesky)/cholesky | solution.py:11
  218.7 9.8 %custom-call.69 = f32[1,128,128]{1,2,0:T(8,128)S(1)} custom-call(f32[1,128,128]{2,1,0:T(8,128)S(1)} %get-tuple-element.35), custom_call_target="InvertDiagBlocksLowerTriangular" | custom-call | tf_op jit(solution)/shard_map/jit(cholesky)/cholesky | solution.py:11
  229.6 2.4 convolution_subtract_fusion.3
  232.0 11.7 %cholesky.504 = f32[128,128]{1,0:T(8,128)S(1)} custom-call(f32[128,128]{1,0:T(8,128)S(1)} %cholesky.596), custom_call_target="Cholesky" | custom-call | tf_op jit(solution)/shard_map/jit(cholesky)/cholesky | solution.py:11
  244.4 10.2 %custom-call.70 = f32[1,128,128]{1,2,0:T(8,128)S(1)} custom-call(f32[1,128,128]{2,1,0:T(8,128)S(1)} %get-tuple-element.32), custom_call_target="InvertDiagBlocksLowerTriangular" | custom-call | tf_op jit(solution)/shard_map/jit(cholesky)/cholesky | solution.py:11
  255.6 2.3 convolution_subtract_fusion.4
  257.9 11.7 %cholesky.524 = f32[128,128]{1,0:T(8,128)S(1)} custom-call(f32[128,128]{1,0:T(8,128)S(1)} %cholesky.601), custom_call_target="Cholesky" | custom-call | tf_op jit(solution)/shard_map/jit(cholesky)/cholesky | solution.py:11
  270.2 9.8 %custom-call.71 = f32[1,128,128]{1,2,0:T(8,128)S(1)} custom-call(f32[1,128,128]{2,1,0:T(8,128)S(1)} %get-tuple-element.29), custom_call_target="InvertDiagBlocksLowerTriangular" | custom-call | tf_op jit(solution)/shard_map/jit(cholesky)/cholesky | solution.py:11
  281.0 2.0 convolution_subtract_fusion.5
  283.0 11.9 %cholesky.544 = f32[128,128]{1,0:T(8,128)S(1)} custom-call(f32[128,128]{1,0:T(8,128)S(1)} %cholesky.606), custom_call_target="Cholesky" | custom-call | tf_op jit(solution)/shard_map/jit(cholesky)/cholesky | solution.py:11
  295.5 9.8 %custom-call.72 = f32[1,128,128]{1,2,0:T(8,128)S(1)} custom-call(f32[1,128,128]{2,1,0:T(8,128)S(1)} %get-tuple-element.26), custom_call_target="InvertDiagBlocksLowerTriangular" | custom-call | tf_op jit(solution)/shard_map/jit(cholesky)/cholesky | solution.py:11
  306.2 1.8 convolution_subtract_fusion.6
  308.0 11.7 %cholesky.562 = f32[128,128]{1,0:T(8,128)S(1)} custom-call(f32[128,128]{1,0:T(8,128)S(1)} %convolution_subtract_fusion.6), custom_call_target="Cholesky" | custom-call | tf_op jit(solution)/shard_map/jit(cholesky)/cholesky | solution.py:11
  329.9 4.8 select_select_fusion
  334.7 22.5 %while.1 = (s32[]{:T(128)}, f32[1024,1024]{1,0:T(8,128)}, s32[8,2]{0,1:T(2,128)S(1)}, f32[8,128,128]{2,1,0:T(8,128)S(1)}, s32[]{:T(128)}) while((s32[]{:T(128)}, f32[1024,1024]{1,0:T(8,128)}, s32[8,2]{0,1:T(2,128)S(1)}, f32[8,128,128]{2,1,0:T(8,128)S(1)}, s32[]{:T(128)}) %tuple.56), condition=%wide.while_cond, body=%wide.while_body.sunk | while | flops 2 | bytes 131189 | solution.py:13
  335.3 2.2 bitcast_dynamic-update-slice_fusion.2
  338.1 2.2 bitcast_dynamic-update-slice_fusion.2
  340.9 2.2 bitcast_dynamic-update-slice_fusion.2
  343.8 2.2 bitcast_dynamic-update-slice_fusion.2
  346.6 2.2 bitcast_dynamic-update-slice_fusion.2
  349.4 2.2 bitcast_dynamic-update-slice_fusion.2
  352.2 2.2 bitcast_dynamic-update-slice_fusion.2
  355.0 2.1 bitcast_dynamic-update-slice_fusion.2
  357.2 78.8 %custom-call.73 = f32[8,128,128]{1,2,0:T(8,128)S(1)} custom-call(f32[8,128,128]{2,1,0:T(8,128)S(1)} %get-tuple-element.12), custom_call_target="InvertDiagBlocksLowerTriangular" | custom-call | tf_op jit(solution)/shard_map/jit(_solve_triangular)/triangular_solve | solution.py:13
  436.0 365.3 %reduce-scatter.5.cloned.1.call-done = f32[8,1024]{1,0:T(8,128)} async-done(((f32[1024,1024]{1,0:T(8,128)}), f32[8,1024]{1,0:T(8,128)}) %reduce-scatter.5.cloned.1.call-update) | async-done | bytes 32784 | tf_op jit(solution)/shard_map/reduce_scatter | solution.py:27
  809.1 1.4 convolution_subtract_fusion.20
  810.6 1.5 convolution_subtract_fusion.19
  823.0 70.4 %psum.7 = f32[1024]{0:T(1024)S(1)} all-reduce(f32[1024]{0:T(1024)S(1)} %multiply_reduce_fusion), channel_id=1, replica_groups=mesh['dp'=32,'tensor'=4] {'dp','tensor'}, use_global_device_ids=true, to_apply=%region_19.20 | all-reduce | flops 1024 | bytes 8192 | tf_op jit(solution)/shard_map/psum | solution.py:38
  (111 shorter events, 40.4 us)
Async XLA Ops:
  7.4 92.3 %all-gather.2.cloned.1.call-start = ((), (), s32[]{:S(2)}) async-start(), calls=%async_computation.2 | async-start | bytes 2113536 | tf_op jit(solution)/shard_map/all_gather | solution.py:24
  8.1 152.6 %reduce-scatter.3.cloned.1.call-start = ((), (), s32[]{:S(2)}) async-start(), calls=%async_computation.3 | async-start | bytes 5242880 | tf_op jit(solution)/shard_map/reduce_scatter | solution.py:18
  21.9 779.3 %reduce-scatter.5.cloned.1.call-start = ((), (), s32[]{:S(2)}) async-start(), calls=%async_computation.4 | async-start | bytes 4227072 | tf_op jit(solution)/shard_map/reduce_scatter | solution.py:27
  104.2 2.0 copy-start
  118.9 2.0 copy-start.1
  120.8 39.9 %copy-start.2 = (bf16[1024,1024]{1,0:T(8,128)(2,1)S(1)}, bf16[1024,1024]{1,0:T(8,128)(2,1)}, u32[]{:S(2)}) copy-start(bf16[1024,1024]{1,0:T(8,128)(2,1)} %all-gather.2.cloned.1.call-done) | copy-start | bytes 6291460
Sparse Core Ops, SparseCore 0:
  11.2 88.4 all-gather.1
  166.7 634.4 reduce-scatter.4
Sparse Core Ops, SparseCore 1:
  22.0 50.3 reduce-scatter.2
where the time goes:
time: 908 us; the launch traced here: 902 us
  waiting for transfers between devices  444 us (49%)
  other arithmetic  263 us (29%)
  blocking collectives  70.4 us (8%)
  matrix products  68.9 us (8%)
  local copies, waits for them, and re-layouts  34.8 us (4%)
  between operations  20.4 us (2%)
    reduce_scatter x1, waiting for transfers between devices, shards(): lax.psum_scatter(lax.dot_general(summed, squared, (((0,), (0,)), ((), ())...  365 us
    another operation x30, other arithmetic, solve_rows(): lower = jnp.linalg.cholesky(hadamard)  172 us
    another operation x3, other arithmetic, solve_rows(): jax.scipy.linalg.solve_triangular(lower, first, lower=True, trans=1)  83.6 us
    all_gather x1, waiting for transfers between devices, shards(): whole_factor = lax.all_gather(factor, ('dp', 'tensor'), axis=0, tiled=True)  77.6 us
    psum x1, blocking collectives, shards(): lax.psum(jnp.sum(updated * updated, axis=0), ('dp', 'tensor'))  70.4 us
    another operation x14, matrix products, solve_rows(): lower = jnp.linalg.cholesky(hadamard)  23.3 us
    another operation x24, local copies, waits for them, and re-layouts  22.3 us
  transfers between devices with their start and end apart: 3, of which 2 were waited for; matrix products, arithmetic and copies ran while one was open for 37% of the time, Pallas kernels for 0%

commit v1 on v0

--- a/solution.py
+++ b/solution.py
@@ -35,7 +35,9 @@
     gram = jnp.dot(whole_factor.T, whole_factor, preferred_element_type=jnp.float32)
     hadamard = gram * gram + ridge_shift * jnp.eye(gram.shape[0], dtype=jnp.float32)
     updated = solve_rows(moment_rows, hadamard)
-    column_total = lax.psum(jnp.sum(updated * updated, axis=0), ("dp", "tensor"))
+    column_total = jnp.sum(
+        lax.all_gather(jnp.sum(updated * updated, axis=0), ("dp", "tensor")), axis=0
+    )
     scale = jnp.sqrt(column_total / whole_factor.shape[0] + epsilon)
     return updated / scale[None, :]
 

time: 908 us -> 896 us (0.987)
  blocking collectives: 70.4 us -> 58 us
    psum x1 -> x0, blocking collectives: 70.4 us -> none  [shards(): lax.psum(jnp.sum(updated * updated, axis=0), ('dp', 'tensor'))]
    all_gather x0 -> x1, blocking collectives: none -> 58 us  [shards(): lax.all_gather(jnp.sum(updated * updated, axis=0), ('dp', 'tensor'))]
  transfers between devices with their start and end apart: 3 -> 3, of which waited for: 2 -> 2; matrix products, arithmetic and copies ran while one was open for 37% -> 38% of each run, Pallas kernels for 0% -> 0%
where the time goes in v1:
time: 896 us; the launch traced here: 889 us
  waiting for transfers between devices  444 us (50%)
  other arithmetic  264 us (29%)
  matrix products  68.7 us (8%)
  blocking collectives  58 us (6%)
  local copies, waits for them, and re-layouts  34.7 us (4%)
  between operations  20.4 us (2%)
    reduce_scatter x1, waiting for transfers between devices, shards(): lax.psum_scatter(lax.dot_general(summed, squared, (((0,), (0,)), ((), ())...  365 us
    another operation x30, other arithmetic, solve_rows(): lower = jnp.linalg.cholesky(hadamard)  172 us
    another operation x3, other arithmetic, solve_rows(): jax.scipy.linalg.solve_triangular(lower, first, lower=True, trans=1)  83.6 us
    all_gather x1, waiting for transfers between devices, shards(): whole_factor = lax.all_gather(factor, ('dp', 'tensor'), axis=0, tiled=True)  77.6 us
    all_gather x1, blocking collectives, shards(): lax.all_gather(jnp.sum(updated * updated, axis=0), ('dp', 'tensor'))  58 us
    another operation x14, matrix products, solve_rows(): lower = jnp.linalg.cholesky(hadamard)  23.3 us
    another operation x24, local copies, waits for them, and re-layouts  22.3 us
  transfers between devices with their start and end apart: 3, of which 2 were waited for; matrix products, arithmetic and copies ran while one was open for 38% of the time, Pallas kernels for 0%

profile of v1, /device:TPU:1, one launch (start us, length us, event | category | flops | bytes accessed | tf_op | source)
XLA Modules:
  0.0 889.4 jit_solution(5222833926832703643)
XLA Ops:
  8.1 13.8 %convolution_convert_fusion = bf16[2048,1024]{1,0:T(8,128)(2,1)} fusion(bf16[2048,2048]{1,0:T(8,128)(2,1)} %param.3, bf16[2048,1024]{1,0:T(8,128)(2,1)} %param.4), kind=kOutput, calls=%fused_computation.8 | convolution fusion | flops 8592031744 | bytes 16777216 | tf_op jit(solution)/shard_map/dot_general | solution.py:19
  22.0 77.6 %all-gather.3.cloned.1.call-done = bf16[1024,1024]{1,0:T(8,128)(2,1)} async-done(((bf16[8,1024]{1,0:T(8,128)(2,1)}), bf16[1024,1024]{1,0:T(8,128)(2,1)}) %all-gather.3.cloned.1.call-update) | async-done | bytes 2097168 | tf_op jit(solution)/shard_map/all_gather | solution.py:24
  99.6 4.6 fusion.95
  104.3 2.0 copy-done
  106.2 2.4 multiply_bitcast_fusion
  108.6 5.6 copy.6
  114.2 4.5 add_multiply_fusion
  118.7 2.0 copy-done.1
  120.7 11.7 %cholesky.222 = f32[128,128]{1,0:T(8,128)S(1)} custom-call(f32[128,128]{1,0:T(8,128)S(1)} %cholesky.577), custom_call_target="Cholesky" | custom-call | tf_op jit(solution)/shard_map/jit(cholesky)/cholesky | solution.py:11
  132.4 2.5 cholesky.254
  134.9 9.8 %custom-call.66 = f32[1,128,128]{1,2,0:T(8,128)S(1)} custom-call(f32[1,128,128]{2,1,0:T(8,128)S(1)} %get-tuple-element.44), custom_call_target="InvertDiagBlocksLowerTriangular" | custom-call | tf_op jit(solution)/shard_map/jit(cholesky)/cholesky | solution.py:11
  144.7 2.3 constant_dynamic-update-slice_fusion.50
  147.1 1.5 convolution_subtract_fusion
  148.7 12.2 %cholesky.243 = f32[128,128]{1,0:T(8,128)S(1)} custom-call(f32[128,128]{1,0:T(8,128)S(1)} %cholesky.581), custom_call_target="Cholesky" | custom-call | tf_op jit(solution)/shard_map/jit(cholesky)/cholesky | solution.py:11
  160.9 5.9 fusion.1
  167.4 9.8 %custom-call.67 = f32[1,128,128]{1,2,0:T(8,128)S(1)} custom-call(f32[1,128,128]{2,1,0:T(8,128)S(1)} %get-tuple-element.41), custom_call_target="InvertDiagBlocksLowerTriangular" | custom-call | tf_op jit(solution)/shard_map/jit(cholesky)/cholesky | solution.py:11
  178.5 2.1 convolution_subtract_fusion.1
  180.6 11.7 %cholesky.466 = f32[128,128]{1,0:T(8,128)S(1)} custom-call(f32[128,128]{1,0:T(8,128)S(1)} %cholesky.586), custom_call_target="Cholesky" | custom-call | tf_op jit(solution)/shard_map/jit(cholesky)/cholesky | solution.py:11
  193.0 9.8 %custom-call.68 = f32[1,128,128]{1,2,0:T(8,128)S(1)} custom-call(f32[1,128,128]{2,1,0:T(8,128)S(1)} %get-tuple-element.38), custom_call_target="InvertDiagBlocksLowerTriangular" | custom-call | tf_op jit(solution)/shard_map/jit(cholesky)/cholesky | solution.py:11
  204.0 2.5 convolution_subtract_fusion.2
  206.5 11.7 %cholesky.485 = f32[128,128]{1,0:T(8,128)S(1)} custom-call(f32[128,128]{1,0:T(8,128)S(1)} %cholesky.591), custom_call_target="Cholesky" | custom-call | tf_op jit(solution)/shard_map/jit(cholesky)/cholesky | solution.py:11
  218.8 9.8 %custom-call.69 = f32[1,128,128]{1,2,0:T(8,128)S(1)} custom-call(f32[1,128,128]{2,1,0:T(8,128)S(1)} %get-tuple-element.35), custom_call_target="InvertDiagBlocksLowerTriangular" | custom-call | tf_op jit(solution)/shard_map/jit(cholesky)/cholesky | solution.py:11
  229.7 2.4 convolution_subtract_fusion.3
  232.1 11.7 %cholesky.504 = f32[128,128]{1,0:T(8,128)S(1)} custom-call(f32[128,128]{1,0:T(8,128)S(1)} %cholesky.596), custom_call_target="Cholesky" | custom-call | tf_op jit(solution)/shard_map/jit(cholesky)/cholesky | solution.py:11
  244.5 10.0 %custom-call.70 = f32[1,128,128]{1,2,0:T(8,128)S(1)} custom-call(f32[1,128,128]{2,1,0:T(8,128)S(1)} %get-tuple-element.32), custom_call_target="InvertDiagBlocksLowerTriangular" | custom-call | tf_op jit(solution)/shard_map/jit(cholesky)/cholesky | solution.py:11
  255.5 2.3 convolution_subtract_fusion.4
  257.8 11.7 %cholesky.524 = f32[128,128]{1,0:T(8,128)S(1)} custom-call(f32[128,128]{1,0:T(8,128)S(1)} %cholesky.601), custom_call_target="Cholesky" | custom-call | tf_op jit(solution)/shard_map/jit(cholesky)/cholesky | solution.py:11
  270.2 9.8 %custom-call.71 = f32[1,128,128]{1,2,0:T(8,128)S(1)} custom-call(f32[1,128,128]{2,1,0:T(8,128)S(1)} %get-tuple-element.29), custom_call_target="InvertDiagBlocksLowerTriangular" | custom-call | tf_op jit(solution)/shard_map/jit(cholesky)/cholesky | solution.py:11
  280.9 2.0 convolution_subtract_fusion.5
  283.0 12.1 %cholesky.544 = f32[128,128]{1,0:T(8,128)S(1)} custom-call(f32[128,128]{1,0:T(8,128)S(1)} %cholesky.606), custom_call_target="Cholesky" | custom-call | tf_op jit(solution)/shard_map/jit(cholesky)/cholesky | solution.py:11
  295.7 9.8 %custom-call.72 = f32[1,128,128]{1,2,0:T(8,128)S(1)} custom-call(f32[1,128,128]{2,1,0:T(8,128)S(1)} %get-tuple-element.26), custom_call_target="InvertDiagBlocksLowerTriangular" | custom-call | tf_op jit(solution)/shard_map/jit(cholesky)/cholesky | solution.py:11
  306.4 1.8 convolution_subtract_fusion.6
  308.2 11.7 %cholesky.562 = f32[128,128]{1,0:T(8,128)S(1)} custom-call(f32[128,128]{1,0:T(8,128)S(1)} %convolution_subtract_fusion.6), custom_call_target="Cholesky" | custom-call | tf_op jit(solution)/shard_map/jit(cholesky)/cholesky | solution.py:11
  330.0 4.8 select_select_fusion
  334.9 22.5 %while.1 = (s32[]{:T(128)}, f32[1024,1024]{1,0:T(8,128)}, s32[8,2]{0,1:T(2,128)S(1)}, f32[8,128,128]{2,1,0:T(8,128)S(1)}, s32[]{:T(128)}) while((s32[]{:T(128)}, f32[1024,1024]{1,0:T(8,128)}, s32[8,2]{0,1:T(2,128)S(1)}, f32[8,128,128]{2,1,0:T(8,128)S(1)}, s32[]{:T(128)}) %tuple.56), condition=%wide.while_cond, body=%wide.while_body.sunk | while | flops 2 | bytes 131189 | solution.py:13
  335.5 2.2 bitcast_dynamic-update-slice_fusion.2
  338.3 2.2 bitcast_dynamic-update-slice_fusion.2
  341.1 2.2 bitcast_dynamic-update-slice_fusion.2
  343.9 2.2 bitcast_dynamic-update-slice_fusion.2
  346.8 2.2 bitcast_dynamic-update-slice_fusion.2
  349.6 2.2 bitcast_dynamic-update-slice_fusion.2
  352.4 2.2 bitcast_dynamic-update-slice_fusion.2
  355.2 2.1 bitcast_dynamic-update-slice_fusion.2
  357.4 78.8 %custom-call.73 = f32[8,128,128]{1,2,0:T(8,128)S(1)} custom-call(f32[8,128,128]{2,1,0:T(8,128)S(1)} %get-tuple-element.12), custom_call_target="InvertDiagBlocksLowerTriangular" | custom-call | tf_op jit(solution)/shard_map/jit(_solve_triangular)/triangular_solve | solution.py:13
  436.1 365.3 %reduce-scatter.5.cloned.1.call-done = f32[8,1024]{1,0:T(8,128)} async-done(((f32[1024,1024]{1,0:T(8,128)}), f32[8,1024]{1,0:T(8,128)}) %reduce-scatter.5.cloned.1.call-update) | async-done | bytes 32784 | tf_op jit(solution)/shard_map/reduce_scatter | solution.py:27
  809.3 1.4 convolution_subtract_fusion.20
  810.9 1.6 convolution_subtract_fusion.19
  823.0 58.0 %all-gather = f32[131072]{0:T(1024)S(1)} all-gather(f32[1024]{0:T(1024)S(1)} %multiply_reduce_fusion), channel_id=2, replica_groups=mesh['dp'=32,'tensor'=4] {'dp','tensor'}, dimensions={0}, use_global_device_ids=true | all-gather | bytes 528384 | tf_op jit(solution)/shard_map/all_gather | solution.py:39
  (113 shorter events, 40.4 us)
Async XLA Ops:
  7.4 92.3 %all-gather.3.cloned.1.call-start = ((), (), s32[]{:S(2)}) async-start(), calls=%async_computation.2 | async-start | bytes 2113536 | tf_op jit(solution)/shard_map/all_gather | solution.py:24
  8.1 152.8 %reduce-scatter.3.cloned.1.call-start = ((), (), s32[]{:S(2)}) async-start(), calls=%async_computation.3 | async-start | bytes 5242880 | tf_op jit(solution)/shard_map/reduce_scatter | solution.py:18
  21.9 779.5 %reduce-scatter.5.cloned.1.call-start = ((), (), s32[]{:S(2)}) async-start(), calls=%async_computation.4 | async-start | bytes 4227072 | tf_op jit(solution)/shard_map/reduce_scatter | solution.py:27
  104.2 2.0 copy-start
  118.7 2.0 copy-start.1
  120.7 40.2 %copy-start.2 = (bf16[1024,1024]{1,0:T(8,128)(2,1)S(1)}, bf16[1024,1024]{1,0:T(8,128)(2,1)}, u32[]{:S(2)}) copy-start(bf16[1024,1024]{1,0:T(8,128)(2,1)} %all-gather.3.cloned.1.call-done) | copy-start | bytes 6291460
Sparse Core Ops, SparseCore 0:
  11.2 88.4 all-gather.2
  166.9 634.5 reduce-scatter.4
Sparse Core Ops, SparseCore 1:
  22.0 50.3 reduce-scatter.2
